TPU v7x, 32 devices: a whole 2x2x4 slice. The times are simulated.
32 devices in a mesh: section: 4 (over z), dp: 4 (over x, core), tensor: 2 (over y).
Axes of the slice: x: 2, y: 2, z: 4, core: 2. Of those that a mesh axis runs over, the one named last changes fastest.
Arguments:
- activations: bfloat16 [4, 512, 4096], P('section', 'dp', 'tensor'), may hold values from -32 to 32
- norm_gain: float32 [4, 4096], P('section', 'tensor'), may hold values from 0.5 to 2
- weights: bfloat16 [4, 4096, 1024], P('section', 'tensor'), may hold values from -0.09375 to 0.09375
- cotangent: bfloat16 [4, 512, 1024], P('section', 'dp'), may hold values from -16 to 16
- top_grad: bfloat16 [512, 4096], P('dp', 'tensor'), may hold values from -6 to 6
- owner_slot: int32 [4, 2, 13], P('section', 'tensor'), may hold values from 0 to 15, as said below
- sweeps: int32 [4, 2, 4], P('section', 'tensor'), may hold values from 3 to 6
Outputs:
- input_grad: bfloat16 [4, 512, 4096], P('section', 'dp', 'tensor')
- preconditioned: bfloat16 [4, 4096, 1024], P('section', 'tensor')
Inputs may be any that keep to these rules, and one draw needn't show every extreme that they name: For each section and tensor index the 13 entries are distinct; the unit is owned by data replica owner_slot // 4, so a replica owns at most 4 units, and some replica owns exactly 4.
All inputs are finite; a program needn't handle non-finite values.
Results may differ from a plain program's by a relative error of at most 0.035.
Values may be sent and summed in bfloat16 or wider, within the bound.
No kernel may reach another device: no remote copies, remote signals or barrier semaphores. Data moves between devices by JAX's collectives and lax.ppermute only.
A program may use at most 128 MiB of HBM per device.

v0:
```python
import jax
import jax.numpy as jnp
from jax import lax
from jax.sharding import PartitionSpec as P

BLOCK = 512
ITERS = 6
EPSILON = 1e-05
DAMPING = 0.05
HIGHEST_PREC = lax.Precision.HIGHEST


def entering(value, axis, combine, identity):
    count, index = (lax.axis_size(axis), lax.axis_index(axis))
    everything = lax.all_gather(value.astype(jnp.bfloat16), axis)
    start = jnp.broadcast_to(jnp.asarray(identity, value.dtype), value.shape)

    def turn(k, before):
        at = count - 1 - k
        reached = at > index
        new = combine(before, everything[at].astype(value.dtype))
        return jnp.where(reached, new, before)

    return lax.fori_loop(0, count, turn, start)


def add_arrays(first_part, second_part):
    return first_part + second_part


def newton_schulz(matrices, limits):
    order_size = matrices.shape[-1]
    identity = jnp.eye(order_size, dtype=jnp.float32)
    frobenius = jnp.sqrt(jnp.sum(matrices * matrices, axis=(1, 2)))
    approx = identity[None] / frobenius[:, None, None]
    for each_sweep in range(ITERS):
        product = jnp.einsum("cij,cjk->cik", matrices, approx, precision=HIGHEST_PREC)
        update = jnp.einsum(
            "cij,cjk->cik", approx, 2.0 * identity[None] - product, precision=HIGHEST_PREC
        )
        approx = jnp.where((each_sweep < limits)[:, None, None], update, approx)
    return approx


def on_device(activations, norm_gain, weights, cotangent, top_grad, owner_slot, sweeps):
    inputs = activations[0].astype(jnp.float32)
    gain_row = norm_gain[0]
    weight_half = weights[0]
    upstream_v = cotangent[0]
    slot_table = owner_slot[0, 0]
    replica_limits = sweeps[0, 0]
    token_count, half_width = inputs.shape
    value_width = weight_half.shape[1]
    tensor_size = lax.axis_size("tensor")
    replica_count = lax.axis_size("dp")
    full_width = half_width * tensor_size
    feature_blocks = half_width // BLOCK
    value_blocks = value_width // BLOCK
    unit_count = feature_blocks + 1 + feature_blocks * value_blocks
    capacity = (unit_count + replica_count - 1) // replica_count
    slot_count = capacity * replica_count
    upstream = lax.dot_general(
        upstream_v, weight_half, (((1,), (1,)), ((), ())), preferred_element_type=jnp.float32
    )
    scaled = upstream * gain_row[None]
    own_squares = jnp.sum(inputs * inputs, axis=1)
    own_inner = jnp.sum(scaled * inputs, axis=1)
    squares, inner_sum = lax.psum((own_squares, own_inner), "tensor")
    inverse_rms = lax.rsqrt(squares / full_width + EPSILON)
    normed = (inputs * inverse_rms[:, None] * gain_row[None]).astype(jnp.bfloat16)
    own_term = (
        inverse_rms[:, None] * scaled
        - inputs * (inverse_rms * inverse_rms * inverse_rms * inner_sum / full_width)[:, None]
    )
    later_sum = entering(own_term, "section", add_arrays, jnp.zeros_like(own_term))
    input_grad = (top_grad.astype(jnp.float32) + later_sum + own_term).astype(jnp.bfloat16)[None]
    normed_blocks = normed.reshape(token_count, feature_blocks, BLOCK)
    value_parts = upstream_v.reshape(token_count, value_blocks, BLOCK)
    feature_units = jnp.einsum(
        "tia,tib->iab", normed_blocks, normed_blocks, preferred_element_type=jnp.float32
    )
    tensor_rank = lax.axis_index("tensor")
    own_values = lax.dynamic_slice_in_dim(upstream_v, tensor_rank * BLOCK, BLOCK, 1)
    value_unit = lax.dot_general(
        own_values, own_values, (((0,), (0,)), ((), ())), preferred_element_type=jnp.float32
    )
    grad_units = jnp.einsum(
        "tia,tjb->ijab", normed_blocks, value_parts, preferred_element_type=jnp.float32
    )
    grad_units = grad_units.reshape(feature_blocks * value_blocks, BLOCK, BLOCK)
    all_units = jnp.concatenate([feature_units, value_unit[None], grad_units], axis=0)
    slot_ids = jnp.arange(slot_count, dtype=jnp.int32)
    unit_ids = jnp.arange(unit_count, dtype=jnp.int32)
    matches = slot_table[None, :] == slot_ids[:, None]
    slot_unit = jnp.sum(jnp.where(matches, unit_ids[None, :] + 1, 0), axis=1) - 1
    filled = slot_unit >= 0
    packed = jnp.where(
        filled[:, None, None], jnp.take(all_units, jnp.maximum(slot_unit, 0), axis=0), 0.0
    )
    summed = lax.psum_scatter(
        packed.astype(jnp.bfloat16), "dp", scatter_dimension=0, tiled=True
    ).astype(jnp.float32)
    replica_rank = lax.axis_index("dp")
    first_slot = replica_rank * capacity
    own_units = lax.dynamic_slice_in_dim(slot_unit, first_slot, capacity, 0)
    is_factor = (own_units >= 0) & (own_units <= feature_blocks)
    identity = jnp.eye(BLOCK, dtype=jnp.float32)
    matrices = jnp.where(
        is_factor[:, None, None],
        summed / (token_count * replica_count) + DAMPING * identity[None],
        identity[None],
    )
    own_limit = lax.dynamic_slice_in_dim(replica_limits, replica_rank, 1, 0)
    own_limits = jnp.broadcast_to(own_limit, (capacity,))
    inverses = newton_schulz(matrices, own_limits)
    owned_blocks = jnp.where(is_factor[:, None, None], inverses, summed).astype(jnp.bfloat16)
    gathered = lax.all_gather(owned_blocks, "dp", axis=0, tiled=True)
    value_inverse = jnp.take(gathered, slot_table[feature_blocks], axis=0)
    value_inverses = lax.all_gather(value_inverse[None], "tensor", axis=0, tiled=True)
    feature_all = jnp.take(gathered, slot_table[:feature_blocks], axis=0)
    grad_all = jnp.take(gathered, slot_table[feature_blocks + 1 :], axis=0)
    grad_all = grad_all.reshape(feature_blocks, value_blocks, BLOCK, BLOCK)
    left_part = jnp.einsum(
        "iab,ijbc->ijac", feature_all, grad_all, preferred_element_type=jnp.float32
    ).astype(jnp.bfloat16)
    output = jnp.einsum(
        "ijac,jcd->iajd", left_part, value_inverses, preferred_element_type=jnp.float32
    ).astype(jnp.bfloat16)
    output = output.reshape(half_width, value_width)
    return (input_grad, output[None])


def solution(mesh):
    placed = (
        P("section", "dp", "tensor"),
        P("section", "tensor"),
        P("section", "tensor", None),
        P("section", "dp", None),
        P("dp", "tensor"),
        P("section", "tensor", None),
        P("section", "tensor", None),
    )
    return jax.shard_map(
        on_device,
        mesh=mesh,
        in_specs=placed,
        out_specs=(P("section", "dp", "tensor"), P("section", "tensor", None)),
        check_vma=False,
    )
```

profile of v0, /device:TPU:0, one launch (start us, length us, event | category | flops | bytes accessed | tf_op | source)
XLA Modules:
  0.0 384.0 jit_solution(11449314158731028812)
XLA Ops:
  15.4 5.9 %all-reduce = (f32[128]{0:T(128)S(1)}, f32[128]{0:T(128)S(1)}) all-reduce(f32[128]{0:T(128)S(1)} %get-tuple-element.140, f32[128]{0:T(128)S(1)} %get-tuple-element.139), channel_id=1, replica_groups=mesh['section'=4,'dp'=4,'tensor'=2] {'tensor'}, use_global_device_ids=true, to_apply=%region_3.0 | all-reduce | flops 256 | bytes 2048 | tf_op jit(solution)/shard_map/psum | solution.py:68
  29.0 7.7 %gather_fusion = bf16[16,512,512]{2,1,0:T(8,128)(2,1)} fusion(bf16[13,512,512]{2,1,0:T(8,128)(2,1)} %pad_maximum_fusion, s32[1024]{0:T(1024)S(1)} %pad_clamp_fusion.2), kind=kCustom, calls=%fused_computation | custom fusion | bytes 16777280 | tf_op jit(solution)/shard_map/jit(_take)/gather | solution.py:98
  36.7 9.5 %select_convert_fusion = bf16[16,512,512]{2,1,0:T(8,128)(2,1)} fusion(bf16[16,512,512]{2,1,0:T(8,128)(2,1)} %gather_fusion, pred[16]{0:T(512)(128)(4,1)S(1)} %get-tuple-element.154, pred[16]{0:T(512)(128)(4,1)S(1)} %get-tuple-element.153), kind=kLoop, calls=%fused_computation.4 | loop fusion | flops 8388608 | bytes 16777248 | tf_op jit(solution)/shard_map/convert_element_type | solution.py:101
  51.1 68.4 %reduce-scatter.2.cloned.1.call-done = bf16[4,512,512]{2,1,0:T(8,128)(2,1)} async-done(((bf16[16,512,512]{2,1,0:T(8,128)(2,1)}), bf16[4,512,512]{2,1,0:T(8,128)(2,1)}) %reduce-scatter.2.cloned.1.call-update) | async-done | bytes 2097168 | tf_op jit(solution)/shard_map/reduce_scatter | solution.py:100
  122.5 8.0 %fusion.12 = f32[4,512,512]{2,1,0:T(8,128)S(1)} fusion(bf16[4,512,512]{2,1,0:T(8,128)(2,1)S(1)} %copy-done, f32[4]{0:T(128)S(1)} %sqrt.7, f32[512,512]{1,0:T(8,128)S(1)} %fusion.116, f32[512,512]{1,0:T(8,128)S(1)} %fusion.117, pred[4]{0:T(512)(128)(4,1)S(1)} %compare_and_fusion.2), kind=kOutput, calls=%fused_computation.15 | convolution fusion | flops 6447693824 | bytes 8388628 | tf_op jit(solution)/shard_map/cij,cjk->cik/dot_general | solution.py:37
  130.5 8.5 %divide_select_fusion = f32[4,512,512]{2,1,0:T(8,128)S(1)} fusion(f32[4,512,512]{2,1,0:T(8,128)S(1)} %fusion.12, f32[512,512]{1,0:T(8,128)S(1)} %fusion.115, f32[4]{0:T(128)S(1)} %sqrt.7, f32[512,512]{1,0:T(8,128)S(1)} %fusion.117, pred[]{:T(512)} %bitcast.13), kind=kOutput, calls=%fused_computation.40 | convolution fusion | flops 6446645248 | bytes 10485777 | tf_op jit(solution)/shard_map/cij,cjk->cik/dot_general | solution.py:38
  139.0 7.7 %fusion.10 = f32[4,512,512]{2,1,0:T(8,128)S(1)} fusion(f32[4,512,512]{2,1,0:T(8,128)S(1)} %divide_select_fusion, bf16[4,512,512]{2,1,0:T(8,128)(2,1)S(1)} %copy-done, f32[512,512]{1,0:T(8,128)S(1)} %fusion.116, f32[512,512]{1,0:T(8,128)S(1)} %fusion.117, pred[4]{0:T(512)(128)(4,1)S(1)} %compare_and_fusion.2), kind=kOutput, calls=%fused_computation.14 | convolution fusion | flops 6446645248 | bytes 12582916 | tf_op jit(solution)/shard_map/cij,cjk->cik/dot_general | solution.py:37
  146.7 8.1 %fusion.45 = f32[4,512,512]{2,1,0:T(8,128)S(1)} fusion(f32[4,512,512]{2,1,0:T(8,128)S(1)} %divide_select_fusion, f32[4,512,512]{2,1,0:T(8,128)S(1)} %fusion.10, f32[512,512]{1,0:T(8,128)S(1)} %fusion.115, pred[]{:T(512)} %bitcast.12), kind=kOutput, calls=%fused_computation.43 | convolution fusion | flops 6444548096 | bytes 13631489 | tf_op jit(solution)/shard_map/cij,cjk->cik/dot_general | solution.py:38
  154.8 7.7 %fusion.8 = f32[4,512,512]{2,1,0:T(8,128)S(1)} fusion(f32[4,512,512]{2,1,0:T(8,128)S(1)} %fusion.45, bf16[4,512,512]{2,1,0:T(8,128)(2,1)S(1)} %copy-done, f32[512,512]{1,0:T(8,128)S(1)} %fusion.116, f32[512,512]{1,0:T(8,128)S(1)} %fusion.117, pred[4]{0:T(512)(128)(4,1)S(1)} %compare_and_fusion.2), kind=kOutput, calls=%fused_computation.13 | convolution fusion | flops 6446645248 | bytes 12582916 | tf_op jit(solution)/shard_map/cij,cjk->cik/dot_general | solution.py:37
  162.5 7.9 %fusion.48 = f32[4,512,512]{2,1,0:T(8,128)S(1)} fusion(f32[4,512,512]{2,1,0:T(8,128)S(1)} %fusion.45, f32[4,512,512]{2,1,0:T(8,128)S(1)} %fusion.8, f32[512,512]{1,0:T(8,128)S(1)} %fusion.115, pred[]{:T(512)} %bitcast.11), kind=kOutput, calls=%fused_computation.44 | convolution fusion | flops 6444548096 | bytes 13631489 | tf_op jit(solution)/shard_map/cij,cjk->cik/dot_general | solution.py:38
  170.4 7.9 %fusion.6 = f32[4,512,512]{2,1,0:T(8,128)S(1)} fusion(f32[4,512,512]{2,1,0:T(8,128)S(1)} %fusion.48, bf16[4,512,512]{2,1,0:T(8,128)(2,1)S(1)} %copy-done, f32[512,512]{1,0:T(8,128)S(1)} %fusion.116, f32[512,512]{1,0:T(8,128)S(1)} %fusion.117, pred[4]{0:T(512)(128)(4,1)S(1)} %compare_and_fusion.2), kind=kOutput, calls=%fused_computation.12 | convolution fusion | flops 6446645248 | bytes 12582916 | tf_op jit(solution)/shard_map/cij,cjk->cik/dot_general | solution.py:37
  178.3 7.7 %fusion.51 = f32[4,512,512]{2,1,0:T(8,128)S(1)} fusion(f32[4,512,512]{2,1,0:T(8,128)S(1)} %fusion.48, f32[4,512,512]{2,1,0:T(8,128)S(1)} %fusion.6, f32[512,512]{1,0:T(8,128)S(1)} %fusion.115, pred[]{:T(512)} %bitcast.10), kind=kOutput, calls=%fused_computation.45 | convolution fusion | flops 6444548096 | bytes 13631489 | tf_op jit(solution)/shard_map/cij,cjk->cik/dot_general | solution.py:38
  186.0 8.1 %fusion.4 = f32[4,512,512]{2,1,0:T(8,128)S(1)} fusion(f32[4,512,512]{2,1,0:T(8,128)S(1)} %fusion.51, bf16[4,512,512]{2,1,0:T(8,128)(2,1)S(1)} %copy-done, f32[512,512]{1,0:T(8,128)S(1)} %fusion.116, f32[512,512]{1,0:T(8,128)S(1)} %fusion.117, pred[4]{0:T(512)(128)(4,1)S(1)} %compare_and_fusion.2), kind=kOutput, calls=%fused_computation.11 | convolution fusion | flops 6446645248 | bytes 12582916 | tf_op jit(solution)/shard_map/cij,cjk->cik/dot_general | solution.py:37
  194.1 7.7 %fusion.54 = f32[4,512,512]{2,1,0:T(8,128)S(1)} fusion(f32[4,512,512]{2,1,0:T(8,128)S(1)} %fusion.51, f32[4,512,512]{2,1,0:T(8,128)S(1)} %fusion.4, f32[512,512]{1,0:T(8,128)S(1)} %fusion.115, pred[]{:T(512)} %bitcast.9), kind=kOutput, calls=%fused_computation.46 | convolution fusion | flops 6444548096 | bytes 13631489 | tf_op jit(solution)/shard_map/cij,cjk->cik/dot_general | solution.py:38
  201.8 7.9 %fusion.2 = f32[4,512,512]{2,1,0:T(8,128)S(1)} fusion(f32[4,512,512]{2,1,0:T(8,128)S(1)} %fusion.54, bf16[4,512,512]{2,1,0:T(8,128)(2,1)S(1)} %copy-done, f32[512,512]{1,0:T(8,128)S(1)} %fusion.116, f32[512,512]{1,0:T(8,128)S(1)} %fusion.117, pred[4]{0:T(512)(128)(4,1)S(1)} %compare_and_fusion.2), kind=kOutput, calls=%fused_computation.10 | convolution fusion | flops 6446645248 | bytes 12582916 | tf_op jit(solution)/shard_map/cij,cjk->cik/dot_general | solution.py:37
  209.7 8.6 %fusion.16 = bf16[4,512,512]{2,1,0:T(8,128)(2,1)} fusion(bf16[4,512,512]{2,1,0:T(8,128)(2,1)S(1)} %copy-done, f32[4,512,512]{2,1,0:T(8,128)S(1)} %fusion.54, f32[4,512,512]{2,1,0:T(8,128)S(1)} %fusion.2, f32[512,512]{1,0:T(8,128)S(1)} %fusion.115, pred[4]{0:T(512)(128)(4,1)S(1)} %compare_and_fusion.2, pred[]{:T(512)} %bitcast.8), kind=kOutput, calls=%fused_computation.18 | convolution fusion | flops 6447693824 | bytes 13631493 | tf_op jit(solution)/shard_map/cij,cjk->cik/dot_general | solution.py:38
  222.5 54.3 %all-gather.5.cloned.1.call-done = bf16[16,512,512]{2,1,0:T(8,128)(2,1)} async-done(((bf16[4,512,512]{2,1,0:T(8,128)(2,1)}), bf16[16,512,512]{2,1,0:T(8,128)(2,1)}) %all-gather.5.cloned.1.call-update) | async-done | bytes 8388624 | tf_op jit(solution)/shard_map/all_gather | solution.py:117
  278.7 45.9 %all-gather.9.cloned.1.call-done = bf16[512,2048]{1,0:T(8,128)(2,1)} async-done(((bf16[128,2048]{1,0:T(8,128)(2,1)}), bf16[512,2048]{1,0:T(8,128)(2,1)}) %all-gather.9.cloned.1.call-update) | async-done | bytes 2097168 | tf_op jit(solution)/shard_map/all_gather | solution.py:15
  324.6 6.7 %while.17 = (s32[]{:T(128)}, f32[128,2048]{1,0:T(8,128)S(1)}, s32[]{:T(128)}, bf16[4,128,2048]{2,1,0:T(8,128)(2,1)}, s32[]{:T(128)}, /*index=5*/s32[]{:T(128)}, s32[]{:T(128)}, s32[]{:T(128)}) while((s32[]{:T(128)}, f32[128,2048]{1,0:T(8,128)S(1)}, s32[]{:T(128)}, bf16[4,128,2048]{2,1,0:T(8,128)(2,1)}, s32[]{:T(128)}, ...), condition=%wide.region_5.6_spmd.clone, body=%wide.region_4.5_spmd.clone.sunk | while | flops 1048584 | bytes 2621603 | solution.py:24
  332.4 6.3 %gather_fusion.1 = bf16[8,512,512]{2,1,0:T(8,128)(2,1)} fusion(bf16[16,512,512]{2,1,0:T(8,128)(2,1)} %all-gather.5.cloned.1.call-done, s32[1024]{0:T(1024)S(1)} %pad_clamp_fusion.1), kind=kCustom, calls=%fused_computation.1 | custom fusion | bytes 8388640 | tf_op jit(solution)/shard_map/jit(_take)/gather | solution.py:121
  338.7 7.3 %copy.34 = bf16[4,2,512,512]{2,3,0,1:T(8,128)(2,1)} copy(bf16[4,2,512,512]{3,2,1,0:T(8,128)(2,1)} %bitcast.101) | data formatting | bytes 8388608 | tf_op jit(solution)/shard_map/jit(_take)/gather | solution.py:121
  350.1 8.2 %convert_bitcast_fusion = bf16[4,512,2,512]{1,3,0,2:T(8,128)(2,1)} fusion(bf16[4,2,512,512]{2,3,0,1:T(8,128)(2,1)} %copy.34, pred[4,2]{0,1:T(4,128)(4,1)S(1)} %copy.33, bf16[4,512,512]{2,1,0:T(8,128)(2,1)S(1)} %gather_fusion.2, pred[4]{0:T(512)(128)(4,1)S(1)} %compare_and_fusion, bf16[2,512,512]{2,1,0:T(8,128)(2,1)} %all-gather.7.cloned.1.call-done), kind=kOutput, calls=%fused_computation.23 | convolution fusion | flops 4302307328 | bytes 11534348 | tf_op jit(solution)/shard_map/ijac,jcd->iajd/dot_general | solution.py:126
  358.3 11.3 %copy.37 = bf16[4,512,2,512]{3,2,1,0:T(2,128)(2,1)} copy(bf16[4,512,2,512]{1,3,0,2:T(8,128)(2,1)} %convert_bitcast_fusion) | data formatting | bytes 8388608 | tf_op jit(solution)/shard_map/convert_element_type | solution.py:128
  369.5 7.7 %broadcast_in_dim_reshape.3 = bf16[1,2048,1024]{2,1,0:T(8,128)(2,1)} reshape(bf16[4,512,2,512]{3,2,1,0:T(2,128)(2,1)} %copy.37) | data formatting | bytes 8388608 | tf_op jit(solution)/shard_map/broadcast_in_dim;reshape | solution.py:130
  (73 shorter events, 36.3 us)
Async XLA Ops:
  7.2 14.2 %copy-start.1 = (bf16[1,128,2048]{2,1,0:T(8,128)(2,1)S(1)}, bf16[1,128,2048]{2,1,0:T(8,128)(2,1)}, u32[]{:S(2)}) copy-start(bf16[1,128,2048]{2,1,0:T(8,128)(2,1)} %param.9) | copy-start | bytes 1572868
  7.2 14.2 %copy-start.7 = (f32[1,2048]{1,0:T(1,128)S(1)}, f32[1,2048]{1,0:T(1,128)}, u32[]{:S(2)}) copy-start(f32[1,2048]{1,0:T(1,128)} %param.10) | copy-start | bytes 24580
  7.2 112.3 %reduce-scatter.2.cloned.1.call-start = ((), (), s32[]{:S(2)}) async-start(), calls=%async_computation.1 | async-start | bytes 10485760 | tf_op jit(solution)/shard_map/reduce_scatter | solution.py:100
  10.5 11.3 %copy-start.5 = (bf16[1,128,1024]{2,1,0:T(8,128)(2,1)S(1)}, bf16[1,128,1024]{2,1,0:T(8,128)(2,1)}, u32[]{:S(2)}) copy-start(bf16[1,128,1024]{2,1,0:T(8,128)(2,1)} %param.12) | copy-start | bytes 786436
  46.2 0.7 copy-start.8
  46.2 230.6 %all-gather.5.cloned.1.call-start = ((), (), s32[]{:S(2)}) async-start(), calls=%async_computation.2 | async-start | bytes 10485760 | tf_op jit(solution)/shard_map/all_gather | solution.py:117
  119.5 3.0 copy-start
  209.7 8.7 %copy-start.2 = (bf16[1,128,2048]{2,1,0:T(8,128)(2,1)S(1)}, bf16[1,128,2048]{2,1,0:T(8,128)(2,1)}, u32[]{:S(2)}) copy-start(bf16[1,128,2048]{2,1,0:T(8,128)(2,1)} %param.9) | copy-start | bytes 1572868
  209.7 8.7 %copy-start.3 = (f32[128,2048]{1,0:T(8,128)S(1)}, f32[128,2048]{1,0:T(8,128)}, u32[]{:S(2)}) copy-start(f32[128,2048]{1,0:T(8,128)} %get-tuple-element.157) | copy-start | bytes 3145732
  218.3 1.2 copy-start.9
  218.3 106.3 %all-gather.9.cloned.1.call-start = ((), (), s32[]{:S(2)}) async-start(), calls=%async_computation.4 | async-start | bytes 2621440 | tf_op jit(solution)/shard_map/all_gather | solution.py:15
  219.5 130.6 %all-gather.7.cloned.1.call-start = ((), (), s32[]{:S(2)}) async-start(), calls=%async_computation.3 | async-start | bytes 1572864 | tf_op jit(solution)/shard_map/all_gather | solution.py:119
  324.6 6.7 %copy-start.4 = (f32[128,2048]{1,0:T(8,128)S(1)}, f32[128,2048]{1,0:T(8,128)}, u32[]{:S(2)}) copy-start(f32[128,2048]{1,0:T(8,128)} %get-tuple-element.157) | copy-start | bytes 3145732
  324.6 6.7 %copy-start.6 = (bf16[128,2048]{1,0:T(8,128)(2,1)S(1)}, bf16[128,2048]{1,0:T(8,128)(2,1)}, u32[]{:S(2)}) copy-start(bf16[128,2048]{1,0:T(8,128)(2,1)} %param.13) | copy-start | bytes 1572868
Sparse Core Ops, SparseCore 0:
  46.3 73.1 reduce-scatter.1
  218.5 58.2 all-gather.4
  278.9 45.6 all-gather.8
  326.0 20.0 all-gather.6
where the time goes:
time: 391 us; the launch traced here: 384 us
  waiting for transfers between devices  169 us (43%)
  matrix products  112 us (29%)
  local copies, waits for them, and re-layouts  48.8 us (12%)
  other arithmetic  29.1 us (7%)
  between operations  19.5 us (5%)
  blocking collectives  5.87 us (2%)
    reduce_scatter x1, waiting for transfers between devices, on_device(): lax.psum_scatter(packed.astype(jnp.bfloat16), 'dp', scatter_dimension=0,...  68.4 us
    all_gather x1, waiting for transfers between devices, on_device(): gathered = lax.all_gather(owned_blocks, 'dp', axis=0, tiled=True)  54.3 us
    dot_general x6, matrix products, newton_schulz(): jnp.einsum('cij,cjk->cik', approx, 2.0 * identity[None] - product, precis...  48.6 us
    dot_general x6, matrix products, newton_schulz(): jnp.einsum('cij,cjk->cik', matrices, approx, precision=HIGHEST_PREC)  47.1 us
    all_gather x1, waiting for transfers between devices, entering(): everything = lax.all_gather(value.astype(jnp.bfloat16), axis)  45.9 us
    gather x2, local copies, waits for them, and re-layouts, on_device(): grad_all = jnp.take(gathered, slot_table[feature_blocks + 1:], axis=0)  13.6 us
    convert_element_type x1, local copies, waits for them, and re-layouts, on_device(): output = jnp.einsum('ijac,jcd->iajd', left_part, value_inverses, preferre...  11.3 us
    convert_element_type x1, other arithmetic, on_device(): packed.astype(jnp.bfloat16)  9.52 us
  transfers between devices with their start and end apart: 4, of which 3 were waited for; matrix products, arithmetic and copies ran while one was open for 8% of the time, Pallas kernels for 0%

commit v1 on v0

--- a/solution.py
+++ b/solution.py
@@ -114,7 +114,19 @@
     own_limits = jnp.broadcast_to(own_limit, (capacity,))
     inverses = newton_schulz(matrices, own_limits)
     owned_blocks = jnp.where(is_factor[:, None, None], inverses, summed).astype(jnp.bfloat16)
-    gathered = lax.all_gather(owned_blocks, "dp", axis=0, tiled=True)
+    count_2, mine, extent = (lax.axis_size("dp"), lax.axis_index("dp"), owned_blocks.shape[0])
+    right = [(i, (i + 1) % count_2) for i in range(count_2)]
+    filled_2 = jnp.zeros(
+        (*owned_blocks.shape[:0], count_2 * extent, *owned_blocks.shape[0 + 1 :]),
+        owned_blocks.dtype,
+    )
+    carried = owned_blocks
+    for step in range(count_2):
+        owner = (mine - step) % count_2
+        filled_2 = lax.dynamic_update_slice_in_dim(filled_2, carried, owner * extent, axis=0)
+        if step < count_2 - 1:
+            carried = lax.ppermute(carried, "dp", right)
+    gathered = filled_2
     value_inverse = jnp.take(gathered, slot_table[feature_blocks], axis=0)
     value_inverses = lax.all_gather(value_inverse[None], "tensor", axis=0, tiled=True)
     feature_all = jnp.take(gathered, slot_table[:feature_blocks], axis=0)

time: 391 us -> 372 us (0.951)
  waiting for transfers between devices: 169 us -> 136 us
  local copies, waits for them, and re-layouts: 48.8 us -> 62 us
    ppermute x0 -> x3, waiting for transfers between devices: none -> 66.6 us  [on_device(): carried = lax.ppermute(carried, 'dp', right)]
    all_gather x1 -> x0, waiting for transfers between devices: 54.3 us -> none  [on_device(): gathered = lax.all_gather(owned_blocks, 'dp', axis=0, tiled=True)]
    all_gather x1, waiting for transfers between devices: 45.9 us -> 0.03 us  [entering(): everything = lax.all_gather(value.astype(jnp.bfloat16), axis)]
    dynamic_update_slice x0 -> x3, local copies, waits for them, and re-layouts: none -> 9.19 us  [on_device(): lax.dynamic_update_slice_in_dim(filled_2, carried, owner * extent, axis=0)]
  transfers between devices with their start and end apart: 4 -> 6, of which waited for: 3 -> 4; matrix products, arithmetic and copies ran while one was open for 8% -> 11% of each run, Pallas kernels for 0% -> 0%
where the time goes in v1:
time: 372 us; the launch traced here: 364 us
  waiting for transfers between devices  136 us (37%)
  matrix products  110 us (30%)
  local copies, waits for them, and re-layouts  62 us (17%)
  other arithmetic  29.1 us (8%)
  between operations  21 us (6%)
  blocking collectives  5.87 us (2%)
    reduce_scatter x1, waiting for transfers between devices, on_device(): lax.psum_scatter(packed.astype(jnp.bfloat16), 'dp', scatter_dimension=0,...  68.9 us
    ppermute x3, waiting for transfers between devices, on_device(): carried = lax.ppermute(carried, 'dp', right)  66.6 us
    dot_general x6, matrix products, newton_schulz(): jnp.einsum('cij,cjk->cik', approx, 2.0 * identity[None] - product, precis...  47.2 us
    dot_general x6, matrix products, newton_schulz(): jnp.einsum('cij,cjk->cik', matrices, approx, precision=HIGHEST_PREC)  47.1 us
    gather x2, local copies, waits for them, and re-layouts, on_device(): grad_all = jnp.take(gathered, slot_table[feature_blocks + 1:], axis=0)  13.6 us
    convert_element_type x1, local copies, waits for them, and re-layouts, on_device(): output = jnp.einsum('ijac,jcd->iajd', left_part, value_inverses, preferre...  11.2 us
    convert_element_type x1, other arithmetic, on_device(): packed.astype(jnp.bfloat16)  9.51 us
    dynamic_update_slice x3, local copies, waits for them, and re-layouts, on_device(): lax.dynamic_update_slice_in_dim(filled_2, carried, owner * extent, axis=0)  9.19 us
  transfers between devices with their start and end apart: 6, of which 4 were waited for; matrix products, arithmetic and copies ran while one was open for 11% of the time, Pallas kernels for 0%

profile of v1, /device:TPU:0, one launch (start us, length us, event | category | flops | bytes accessed | tf_op | source)
XLA Modules:
  0.0 364.4 jit_solution(439650509957769553)
XLA Ops:
  29.9 7.7 %gather_fusion = bf16[16,512,512]{2,1,0:T(8,128)(2,1)} fusion(bf16[13,512,512]{2,1,0:T(8,128)(2,1)} %pad_maximum_fusion, s32[1024]{0:T(1024)S(1)} %pad_clamp_fusion.2), kind=kCustom, calls=%fused_computation | custom fusion | bytes 16777280 | tf_op jit(solution)/shard_map/jit(_take)/gather | solution.py:98
  37.5 9.5 %select_convert_fusion = bf16[16,512,512]{2,1,0:T(8,128)(2,1)} fusion(bf16[16,512,512]{2,1,0:T(8,128)(2,1)} %gather_fusion, pred[16]{0:T(512)(128)(4,1)S(1)} %get-tuple-element.154, pred[16]{0:T(512)(128)(4,1)S(1)} %get-tuple-element.153), kind=kLoop, calls=%fused_computation.4 | loop fusion | flops 8388608 | bytes 16777248 | tf_op jit(solution)/shard_map/convert_element_type | solution.py:101
  51.5 68.9 %reduce-scatter.2.cloned.1.call-done = bf16[4,512,512]{2,1,0:T(8,128)(2,1)} async-done(((bf16[16,512,512]{2,1,0:T(8,128)(2,1)}), bf16[4,512,512]{2,1,0:T(8,128)(2,1)}) %reduce-scatter.2.cloned.1.call-update) | async-done | bytes 2097168 | tf_op jit(solution)/shard_map/reduce_scatter | solution.py:100
  123.4 8.0 %fusion.12 = f32[4,512,512]{2,1,0:T(8,128)S(1)} fusion(bf16[4,512,512]{2,1,0:T(8,128)(2,1)S(1)} %copy-done, f32[4]{0:T(128)S(1)} %sqrt.7, f32[512,512]{1,0:T(8,128)S(1)} %fusion.116, f32[512,512]{1,0:T(8,128)S(1)} %fusion.117, pred[4]{0:T(512)(128)(4,1)S(1)} %compare_and_fusion.2), kind=kOutput, calls=%fused_computation.15 | convolution fusion | flops 6447693824 | bytes 8388628 | tf_op jit(solution)/shard_map/cij,cjk->cik/dot_general | solution.py:37
  131.3 8.5 %divide_select_fusion = f32[4,512,512]{2,1,0:T(8,128)S(1)} fusion(f32[4,512,512]{2,1,0:T(8,128)S(1)} %fusion.12, f32[512,512]{1,0:T(8,128)S(1)} %fusion.115, f32[4]{0:T(128)S(1)} %sqrt.7, f32[512,512]{1,0:T(8,128)S(1)} %fusion.117, pred[]{:T(512)} %bitcast.13), kind=kOutput, calls=%fused_computation.40 | convolution fusion | flops 6446645248 | bytes 10485777 | tf_op jit(solution)/shard_map/cij,cjk->cik/dot_general | solution.py:38
  139.8 7.7 %fusion.10 = f32[4,512,512]{2,1,0:T(8,128)S(1)} fusion(f32[4,512,512]{2,1,0:T(8,128)S(1)} %divide_select_fusion, bf16[4,512,512]{2,1,0:T(8,128)(2,1)S(1)} %copy-done, f32[512,512]{1,0:T(8,128)S(1)} %fusion.116, f32[512,512]{1,0:T(8,128)S(1)} %fusion.117, pred[4]{0:T(512)(128)(4,1)S(1)} %compare_and_fusion.2), kind=kOutput, calls=%fused_computation.14 | convolution fusion | flops 6446645248 | bytes 12582916 | tf_op jit(solution)/shard_map/cij,cjk->cik/dot_general | solution.py:37
  147.5 8.0 %fusion.45 = f32[4,512,512]{2,1,0:T(8,128)S(1)} fusion(f32[4,512,512]{2,1,0:T(8,128)S(1)} %divide_select_fusion, f32[4,512,512]{2,1,0:T(8,128)S(1)} %fusion.10, f32[512,512]{1,0:T(8,128)S(1)} %fusion.115, pred[]{:T(512)} %bitcast.12), kind=kOutput, calls=%fused_computation.43 | convolution fusion | flops 6444548096 | bytes 13631489 | tf_op jit(solution)/shard_map/cij,cjk->cik/dot_general | solution.py:38
  155.5 7.7 %fusion.8 = f32[4,512,512]{2,1,0:T(8,128)S(1)} fusion(f32[4,512,512]{2,1,0:T(8,128)S(1)} %fusion.45, bf16[4,512,512]{2,1,0:T(8,128)(2,1)S(1)} %copy-done, f32[512,512]{1,0:T(8,128)S(1)} %fusion.116, f32[512,512]{1,0:T(8,128)S(1)} %fusion.117, pred[4]{0:T(512)(128)(4,1)S(1)} %compare_and_fusion.2), kind=kOutput, calls=%fused_computation.13 | convolution fusion | flops 6446645248 | bytes 12582916 | tf_op jit(solution)/shard_map/cij,cjk->cik/dot_general | solution.py:37
  163.1 7.7 %fusion.48 = f32[4,512,512]{2,1,0:T(8,128)S(1)} fusion(f32[4,512,512]{2,1,0:T(8,128)S(1)} %fusion.45, f32[4,512,512]{2,1,0:T(8,128)S(1)} %fusion.8, f32[512,512]{1,0:T(8,128)S(1)} %fusion.115, pred[]{:T(512)} %bitcast.11), kind=kOutput, calls=%fused_computation.44 | convolution fusion | flops 6444548096 | bytes 13631489 | tf_op jit(solution)/shard_map/cij,cjk->cik/dot_general | solution.py:38
  170.9 7.9 %fusion.6 = f32[4,512,512]{2,1,0:T(8,128)S(1)} fusion(f32[4,512,512]{2,1,0:T(8,128)S(1)} %fusion.48, bf16[4,512,512]{2,1,0:T(8,128)(2,1)S(1)} %copy-done, f32[512,512]{1,0:T(8,128)S(1)} %fusion.116, f32[512,512]{1,0:T(8,128)S(1)} %fusion.117, pred[4]{0:T(512)(128)(4,1)S(1)} %compare_and_fusion.2), kind=kOutput, calls=%fused_computation.12 | convolution fusion | flops 6446645248 | bytes 12582916 | tf_op jit(solution)/shard_map/cij,cjk->cik/dot_general | solution.py:37
  178.8 7.6 %fusion.51 = f32[4,512,512]{2,1,0:T(8,128)S(1)} fusion(f32[4,512,512]{2,1,0:T(8,128)S(1)} %fusion.48, f32[4,512,512]{2,1,0:T(8,128)S(1)} %fusion.6, f32[512,512]{1,0:T(8,128)S(1)} %fusion.115, pred[]{:T(512)} %bitcast.10), kind=kOutput, calls=%fused_computation.45 | convolution fusion | flops 6444548096 | bytes 13631489 | tf_op jit(solution)/shard_map/cij,cjk->cik/dot_general | solution.py:38
  186.4 8.1 %fusion.4 = f32[4,512,512]{2,1,0:T(8,128)S(1)} fusion(f32[4,512,512]{2,1,0:T(8,128)S(1)} %fusion.51, bf16[4,512,512]{2,1,0:T(8,128)(2,1)S(1)} %copy-done, f32[512,512]{1,0:T(8,128)S(1)} %fusion.116, f32[512,512]{1,0:T(8,128)S(1)} %fusion.117, pred[4]{0:T(512)(128)(4,1)S(1)} %compare_and_fusion.2), kind=kOutput, calls=%fused_computation.11 | convolution fusion | flops 6446645248 | bytes 12582916 | tf_op jit(solution)/shard_map/cij,cjk->cik/dot_general | solution.py:37
  194.5 7.8 %fusion.54 = f32[4,512,512]{2,1,0:T(8,128)S(1)} fusion(f32[4,512,512]{2,1,0:T(8,128)S(1)} %fusion.51, f32[4,512,512]{2,1,0:T(8,128)S(1)} %fusion.4, f32[512,512]{1,0:T(8,128)S(1)} %fusion.115, pred[]{:T(512)} %bitcast.9), kind=kOutput, calls=%fused_computation.46 | convolution fusion | flops 6444548096 | bytes 13631489 | tf_op jit(solution)/shard_map/cij,cjk->cik/dot_general | solution.py:38
  202.3 7.8 %fusion.2 = f32[4,512,512]{2,1,0:T(8,128)S(1)} fusion(f32[4,512,512]{2,1,0:T(8,128)S(1)} %fusion.54, bf16[4,512,512]{2,1,0:T(8,128)(2,1)S(1)} %copy-done, f32[512,512]{1,0:T(8,128)S(1)} %fusion.116, f32[512,512]{1,0:T(8,128)S(1)} %fusion.117, pred[4]{0:T(512)(128)(4,1)S(1)} %compare_and_fusion.2), kind=kOutput, calls=%fused_computation.10 | convolution fusion | flops 6446645248 | bytes 12582916 | tf_op jit(solution)/shard_map/cij,cjk->cik/dot_general | solution.py:37
  211.0 7.6 %constant_dynamic-update-slice_fusion.3 = (bf16[16,512,512]{2,1,0:T(8,128)(2,1)S(1)}, bf16[4,512,512]{2,1,0:T(8,128)(2,1)S(1)}) fusion(bf16[16,512,512]{2,1,0:T(8,128)(2,1)S(1)} %broadcast_in_dim.160, s32[]{:T(128)S(6)} %select_n.189, bf16[4,512,512]{2,1,0:T(8,128)(2,1)S(1)} %copy-done, f32[4,512,512]{2,1,0:T(8,128)S(1)} %fusion.54, ...), kind=kOutput, calls=%fused_computation.130 | convolution fusion | flops 6447693824 | bytes 19923460 | tf_op jit(solution)/shard_map/cij,cjk->cik/dot_general | solution.py:38
  221.8 25.6 %collective-permute-done = bf16[4,512,512]{2,1,0:T(8,128)(2,1)} collective-permute-done((bf16[4,512,512]{2,1,0:T(8,128)(2,1)S(1)}, bf16[4,512,512]{2,1,0:T(8,128)(2,1)}, u32[]{:S(2)}, u32[]{:S(2)}) %collective-permute-start) | collective-permute-done | bytes 2097184 | tf_op jit(solution)/shard_map/ppermute | solution.py:128
  248.5 24.7 %collective-permute-done.1 = bf16[4,512,512]{2,1,0:T(8,128)(2,1)} collective-permute-done((bf16[4,512,512]{2,1,0:T(8,128)(2,1)}, bf16[4,512,512]{2,1,0:T(8,128)(2,1)}, u32[]{:S(2)}, u32[]{:S(2)}) %collective-permute-start.1) | collective-permute-done | bytes 2097184 | tf_op jit(solution)/shard_map/ppermute | solution.py:128
  282.8 16.4 %collective-permute-done.2 = bf16[4,512,512]{2,1,0:T(8,128)(2,1)} collective-permute-done((bf16[4,512,512]{2,1,0:T(8,128)(2,1)}, bf16[4,512,512]{2,1,0:T(8,128)(2,1)}, u32[]{:S(2)}, u32[]{:S(2)}) %collective-permute-start.2) | collective-permute-done | bytes 2097184 | tf_op jit(solution)/shard_map/ppermute | solution.py:128
  304.1 6.7 %while.17 = (s32[]{:T(128)}, f32[128,2048]{1,0:T(8,128)S(1)}, s32[]{:T(128)}, bf16[4,128,2048]{2,1,0:T(8,128)(2,1)}, s32[]{:T(128)}, /*index=5*/s32[]{:T(128)}, s32[]{:T(128)}, s32[]{:T(128)}) while((s32[]{:T(128)}, f32[128,2048]{1,0:T(8,128)S(1)}, s32[]{:T(128)}, bf16[4,128,2048]{2,1,0:T(8,128)(2,1)}, s32[]{:T(128)}, ...), condition=%wide.region_5.6_spmd.clone, body=%wide.region_4.5_spmd.clone.sunk | while | flops 1048584 | bytes 2621603 | solution.py:24
  311.9 6.3 %gather_fusion.1 = bf16[8,512,512]{2,1,0:T(8,128)(2,1)} fusion(bf16[16,512,512]{2,1,0:T(8,128)(2,1)} %constant_dynamic-update-slice_fusion, s32[1024]{0:T(1024)S(1)} %pad_clamp_fusion.1), kind=kCustom, calls=%fused_computation.1 | custom fusion | bytes 8388640 | tf_op jit(solution)/shard_map/jit(_take)/gather | solution.py:133
  318.2 7.3 %copy.40 = bf16[4,2,512,512]{2,3,0,1:T(8,128)(2,1)} copy(bf16[4,2,512,512]{3,2,1,0:T(8,128)(2,1)} %bitcast.101) | data formatting | bytes 8388608 | tf_op jit(solution)/shard_map/jit(_take)/gather | solution.py:133
  329.6 8.2 %convert_bitcast_fusion = bf16[4,512,2,512]{1,3,0,2:T(8,128)(2,1)} fusion(bf16[4,2,512,512]{2,3,0,1:T(8,128)(2,1)} %copy.40, pred[4,2]{0,1:T(4,128)(4,1)S(1)} %copy.39, bf16[4,512,512]{2,1,0:T(8,128)(2,1)S(1)} %gather_fusion.2, pred[4]{0:T(512)(128)(4,1)S(1)} %compare_and_fusion, bf16[2,512,512]{2,1,0:T(8,128)(2,1)} %all-gather.4.cloned.1.call-done), kind=kOutput, calls=%fused_computation.23 | convolution fusion | flops 4302307328 | bytes 11534348 | tf_op jit(solution)/shard_map/ijac,jcd->iajd/dot_general | solution.py:138
  337.8 11.2 %copy.43 = bf16[4,512,2,512]{3,2,1,0:T(2,128)(2,1)} copy(bf16[4,512,2,512]{1,3,0,2:T(8,128)(2,1)} %convert_bitcast_fusion) | data formatting | bytes 8388608 | tf_op jit(solution)/shard_map/convert_element_type | solution.py:140
  349.0 7.7 %broadcast_in_dim_reshape.3 = bf16[1,2048,1024]{2,1,0:T(8,128)(2,1)} reshape(bf16[4,512,2,512]{3,2,1,0:T(2,128)(2,1)} %copy.43) | data formatting | bytes 8388608 | tf_op jit(solution)/shard_map/broadcast_in_dim;reshape | solution.py:142
  (80 shorter events, 55.6 us)
Async XLA Ops:
  8.0 14.2 %copy-start.2 = (bf16[1,128,2048]{2,1,0:T(8,128)(2,1)S(1)}, bf16[1,128,2048]{2,1,0:T(8,128)(2,1)}, u32[]{:S(2)}) copy-start(bf16[1,128,2048]{2,1,0:T(8,128)(2,1)} %param.9) | copy-start | bytes 1572868
  8.0 14.1 %copy-start.7 = (f32[1,2048]{1,0:T(1,128)S(1)}, f32[1,2048]{1,0:T(1,128)}, u32[]{:S(2)}) copy-start(f32[1,2048]{1,0:T(1,128)} %param.10) | copy-start | bytes 24580
  8.0 112.4 %reduce-scatter.2.cloned.1.call-start = ((), (), s32[]{:S(2)}) async-start(), calls=%async_computation.1 | async-start | bytes 10485760 | tf_op jit(solution)/shard_map/reduce_scatter | solution.py:100
  11.3 11.3 %copy-start.5 = (bf16[1,128,1024]{2,1,0:T(8,128)(2,1)S(1)}, bf16[1,128,1024]{2,1,0:T(8,128)(2,1)}, u32[]{:S(2)}) copy-start(bf16[1,128,1024]{2,1,0:T(8,128)(2,1)} %param.12) | copy-start | bytes 786436
  47.1 0.7 copy-start.8
  47.1 257.0 %all-gather.6.cloned.1.call-start = ((), (), s32[]{:S(2)}) async-start(), calls=%async_computation.3 | async-start | bytes 2621440 | tf_op jit(solution)/shard_map/all_gather | solution.py:15
  120.4 3.0 copy-start
  210.9 36.5 %copy-start.3 = (bf16[1,128,2048]{2,1,0:T(8,128)(2,1)S(1)}, bf16[1,128,2048]{2,1,0:T(8,128)(2,1)}, u32[]{:S(2)}) copy-start(bf16[1,128,2048]{2,1,0:T(8,128)(2,1)} %param.9) | copy-start | bytes 1572868
  210.9 36.5 %copy-start.4 = (f32[128,2048]{1,0:T(8,128)S(1)}, f32[128,2048]{1,0:T(8,128)}, u32[]{:S(2)}) copy-start(f32[128,2048]{1,0:T(8,128)} %get-tuple-element.157) | copy-start | bytes 3145732
  210.9 62.5 %copy-start.9 = (s32[1,1,13]{2,1,0:T(1,128)S(1)}, s32[1,1,13]{2,1,0:T(1,128)}, u32[]{:S(2)}) copy-start(s32[1,1,13]{2,1,0:T(1,128)} %param.14) | copy-start | bytes 160
  218.6 3.2 copy-start.1
  221.8 25.6 %collective-permute-start = (bf16[4,512,512]{2,1,0:T(8,128)(2,1)S(1)}, bf16[4,512,512]{2,1,0:T(8,128)(2,1)}, u32[]{:S(2)}, u32[]{:S(2)}) collective-permute-start(bf16[4,512,512]{2,1,0:T(8,128)(2,1)S(1)} %get-tuple-element.161), channel_id=1, source_target_pairs={{0,2},{2,4},{4,6},{6,0},{1,3},{3,5},{5,7},{7,1},{8,10},{10,12},{12... | collective-permute-start | bytes 6291464 | tf_op jit(solution)/shard_map/ppermute | solution.py:128
  247.4 25.8 %collective-permute-start.1 = (bf16[4,512,512]{2,1,0:T(8,128)(2,1)}, bf16[4,512,512]{2,1,0:T(8,128)(2,1)}, u32[]{:S(2)}, u32[]{:S(2)}) collective-permute-start(bf16[4,512,512]{2,1,0:T(8,128)(2,1)} %collective-permute-done), channel_id=1, source_target_pairs={{0,2},{2,4},{4,6},{6,0},{1,3},{3,5},{5,7},{7,1},{8,10},{10,12},{12... | collective-permute-start | bytes 6291464 | tf_op jit(solution)/shard_map/ppermute | solution.py:128
  248.4 81.1 %all-gather.4.cloned.1.call-start = ((), (), s32[]{:S(2)}) async-start(), calls=%async_computation.2 | async-start | bytes 1572864 | tf_op jit(solution)/shard_map/all_gather | solution.py:131
  273.2 26.0 %collective-permute-start.2 = (bf16[4,512,512]{2,1,0:T(8,128)(2,1)}, bf16[4,512,512]{2,1,0:T(8,128)(2,1)}, u32[]{:S(2)}, u32[]{:S(2)}) collective-permute-start(bf16[4,512,512]{2,1,0:T(8,128)(2,1)} %collective-permute-done.1), channel_id=1, source_target_pairs={{0,2},{2,4},{4,6},{6,0},{1,3},{3,5},{5,7},{7,1},{8,10},{10,12},{12... | collective-permute-start | bytes 6291464 | tf_op jit(solution)/shard_map/ppermute | solution.py:128
  304.1 6.7 %copy-start.6 = (bf16[128,2048]{1,0:T(8,128)(2,1)S(1)}, bf16[128,2048]{1,0:T(8,128)(2,1)}, u32[]{:S(2)}) copy-start(bf16[128,2048]{1,0:T(8,128)(2,1)} %param.13) | copy-start | bytes 1572868
Sparse Core Ops, SparseCore 0:
  47.2 73.1 reduce-scatter.1
Sparse Core Ops, SparseCore 1:
  248.5 46.6 all-gather.5
  304.2 21.2 all-gather.3
